TPU v7x, 512 devices: a whole 4x8x8 slice. The times are simulated.
512 devices in a mesh: section: 8 (over z), row: 16 (over y, core), col: 4 (over x).
Axes of the slice: x: 4, y: 8, z: 8, core: 2. Of those that a mesh axis runs over, the one named last changes fastest.
Arguments:
- image: bfloat16 [128, 256, 1024], P('section', 'row', 'col'), may hold values from -6 to 6
- conv_kernel: float32 [7, 7, 1024], P(None, None, 'col'), may hold values from -0.875 to 0.875
- norm_gain: float32 [1024], P('col'), may hold values from 0.1 to 1.9
- w_in: bfloat16 [1024, 4096], P('row', 'col'), may hold values from -0.1875 to 0.1875
- w_out: bfloat16 [4096, 1024], P('row', 'col'), may hold values from -0.09375 to 0.09375
- upstream: bfloat16 [128, 256, 1024], P('section', 'row', 'col'), may hold values from -6 to 6
Outputs:
- output: bfloat16 [128, 256, 1024], P('section', 'row', 'col')
- image_grad: float32 [128, 256, 1024], P('section', 'row', 'col')
All inputs are finite; a program needn't handle non-finite values.
Results may differ from a plain program's by a relative error of at most 0.0095.
Values may be sent and summed in bfloat16 or wider, within the bound.
A program may use at most 64 MiB of HBM per device.

v0:
```python
import math

import jax
import jax.numpy as jnp
from jax import lax
from jax.sharding import PartitionSpec as P

KERNEL = 7


EPSILON = 1e-06


def extended(block, sides, width):
    for axis, dim in sides:
        count = lax.axis_size(axis)
        forward = [(i, i + 1) for i in range(count - 1)]
        backward = [(target, source) for source, target in forward]
        low = lax.ppermute(
            lax.slice_in_dim(block, block.shape[dim] - width, None, axis=dim), axis, forward
        )
        high = lax.ppermute(lax.slice_in_dim(block, 0, width, axis=dim), axis, backward)
        block = jnp.concatenate([low, block, high], axis=dim)
    return block


def depthwise(padded, kernel, height, breadth, start):
    total = jnp.zeros((height, breadth, padded.shape[2]), jnp.float32)
    for row_off in range(KERNEL):
        for col_off in range(KERNEL):
            lead = start - row_off if start > 0 else row_off
            side = start - col_off if start > 0 else col_off
            total = (
                total
                + padded[lead : lead + height, side : side + breadth, :] * kernel[row_off, col_off]
            )
    return total


def gelu_slope(preact):
    return 0.5 * (1.0 + lax.erf(preact / math.sqrt(2.0))) + preact * jnp.exp(
        -0.5 * preact * preact
    ) / math.sqrt(2.0 * math.pi)


def transposed(left, right):
    return lax.dot_general(
        left, right, (((1,), (1,)), ((), ())), preferred_element_type=jnp.float32
    )


def local(image, conv_kernel, norm_gain, w_in, w_out, upstream):
    height, breadth, chan_local = image.shape
    cells = height * breadth
    margin = KERNEL // 2
    channels_all = chan_local * lax.axis_size("col")
    padded = extended(image, (("section", 0), ("row", 1)), margin)
    mixed = depthwise(padded.astype(jnp.float32), conv_kernel, height, breadth, 0)
    centre = lax.psum(jnp.sum(mixed, axis=-1), "col")[..., None] / channels_all
    centred = mixed - centre
    spread = lax.psum(jnp.sum(centred * centred, axis=-1), "col")[..., None] / channels_all
    inv_std = lax.rsqrt(spread + EPSILON)
    normed = centred * inv_std
    scaled = (normed * norm_gain).astype(jnp.bfloat16).reshape(cells, chan_local)
    features = lax.all_gather(scaled, "col", axis=1, tiled=True)
    columns = features
    preact = jnp.dot(
        columns, lax.all_gather(w_in, "row", axis=0, tiled=True), preferred_element_type=jnp.float32
    )
    hidden = jax.nn.gelu(preact, approximate=False).astype(jnp.bfloat16)
    hidden_all = lax.all_gather(hidden, "col", axis=1, tiled=True)
    columns = hidden_all
    branch = jnp.dot(
        columns,
        lax.all_gather(w_out, "row", axis=0, tiled=True),
        preferred_element_type=jnp.float32,
    )
    flat_image = image.reshape(cells, chan_local).astype(jnp.float32)
    output = (flat_image + branch).astype(jnp.bfloat16).reshape(image.shape)
    grad_flat = upstream.reshape(cells, chan_local)
    hidden_terms = transposed(grad_flat, lax.all_gather(w_out, "row", axis=0, tiled=True))
    hidden_grad = lax.psum_scatter(
        hidden_terms.astype(jnp.bfloat16), "col", scatter_dimension=1, tiled=True
    ).astype(jnp.float32)
    act_grad = (hidden_grad * gelu_slope(preact)).astype(jnp.bfloat16)
    feature_terms = transposed(act_grad, lax.all_gather(w_in, "row", axis=0, tiled=True))
    feature_grad = lax.psum_scatter(
        feature_terms.astype(jnp.bfloat16), "col", scatter_dimension=1, tiled=True
    ).astype(jnp.float32)
    normed_grad = feature_grad.reshape(image.shape) * norm_gain
    grad_first, grad_second = lax.psum(
        (jnp.sum(normed_grad, axis=-1), jnp.sum(normed_grad * normed, axis=-1)), "col"
    )
    mixed_grad = inv_std * (
        normed_grad
        - grad_first[..., None] / channels_all
        - normed * (grad_second[..., None] / channels_all)
    )
    grad_pad = extended(
        mixed_grad.astype(jnp.bfloat16), (("section", 0), ("row", 1)), margin
    ).astype(mixed_grad.dtype)
    image_grad = upstream.astype(jnp.float32) + depthwise(
        grad_pad, conv_kernel, height, breadth, 2 * margin
    )
    return (output, image_grad)


def solution(mesh):
    in_specs = (
        P("section", "row", "col"),
        P(None, None, "col"),
        P("col"),
        P("row", "col"),
        P("row", "col"),
        P("section", "row", "col"),
    )
    out_specs = (P("section", "row", "col"), P("section", "row", "col"))
    return jax.shard_map(local, mesh=mesh, in_specs=in_specs, out_specs=out_specs, check_vma=False)
```

profile of v0, /device:TPU:1, one launch (start us, length us, event | category | flops | bytes accessed | tf_op | source)
XLA Modules:
  0.0 217.5 jit_solution(10997640216240844430)
XLA Ops:
  8.7 49.1 %all-gather.8.cloned.1.call-done = bf16[4096,256]{1,0:T(8,128)(2,1)} async-done(((bf16[256,256]{1,0:T(8,128)(2,1)}), bf16[4096,256]{1,0:T(8,128)(2,1)}) %all-gather.8.cloned.1.call-update) | async-done | bytes 2097168 | tf_op jit(solution)/shard_map/all_gather | solution.py:75
  57.8 3.7 %convolution_convert_fusion = bf16[256,4096]{1,0:T(8,128)(2,1)} fusion(bf16[256,256]{1,0:T(8,128)(2,1)} %bitcast.64, bf16[4096,256]{1,0:T(8,128)(2,1)} %all-gather.8.cloned.1.call-done), kind=kOutput, calls=%fused_computation | convolution fusion | flops 537919488 | bytes 4325376 | tf_op jit(solution)/shard_map/dot_general | solution.py:47
  62.4 3.3 %collective-permute-start = (bf16[3,16,256]{2,1,0:T(8,128)(2,1)S(1)}, bf16[3,16,256]{2,1,0:T(8,128)(2,1)S(1)}, u32[]{:S(2)}, u32[]{:S(2)}) collective-permute-start(bf16[3,16,256]{2,1,0:T(8,128)(2,1)S(1)} %get-tuple-element.13), channel_id=1, source_target_pairs={{0,64},{64,128},{128,192},{192,256},{256,320},{320,384},{384,448},... | collective-permute-start | bytes 73736 | tf_op jit(solution)/shard_map/ppermute | solution.py:19
  65.7 1.3 collective-permute-start.1
  67.1 3.2 %collective-permute-done.1 = bf16[3,16,256]{2,1,0:T(8,128)(2,1)S(1)} collective-permute-done((bf16[3,16,256]{2,1,0:T(8,128)(2,1)S(1)}, bf16[3,16,256]{2,1,0:T(8,128)(2,1)S(1)}, u32[]{:S(2)}, u32[]{:S(2)}) %collective-permute-start.1) | collective-permute-done | bytes 24608 | tf_op jit(solution)/shard_map/ppermute | solution.py:22
  70.3 3.6 %collective-permute-start.3 = (bf16[22,3,256]{2,1,0:T(4,128)(2,1)S(1)}, bf16[22,3,256]{2,1,0:T(4,128)(2,1)S(1)}, u32[]{:S(2)}, u32[]{:S(2)}) collective-permute-start(bf16[22,3,256]{2,1,0:T(4,128)(2,1)S(1)} %get-tuple-element.9), channel_id=1, source_target_pairs={{4,0},{8,4},{12,8},{16,12},{20,16},{24,20},{28,24},{32,28},{36,32}... | collective-permute-start | bytes 101384 | tf_op jit(solution)/shard_map/ppermute | solution.py:22
  73.9 2.7 %collective-permute-start.2 = (bf16[22,3,256]{2,1,0:T(4,128)(2,1)S(1)}, bf16[22,3,256]{2,1,0:T(4,128)(2,1)S(1)}, u32[]{:S(2)}, u32[]{:S(2)}) collective-permute-start(bf16[22,3,256]{2,1,0:T(4,128)(2,1)S(1)} %get-tuple-element.8), channel_id=1, source_target_pairs={{0,4},{4,8},{8,12},{12,16},{16,20},{20,24},{24,28},{28,32},{32,36}... | collective-permute-start | bytes 101384 | tf_op jit(solution)/shard_map/ppermute | solution.py:19
  77.8 1.7 fusion.125
  79.6 9.2 %psum.28 = f32[16,16]{1,0:T(8,128)S(1)} all-reduce(f32[16,16]{1,0:T(8,128)S(1)} %get-tuple-element.4), channel_id=1, replica_groups=mesh['section'=8,'row'=16,'col'=4] {'col'}, use_global_device_ids=true, to_apply=%region_1.0 | all-reduce | flops 256 | bytes 2048 | tf_op jit(solution)/shard_map/psum | solution.py:59
  89.0 6.9 %psum.29 = f32[16,16]{1,0:T(8,128)S(1)} all-reduce(f32[16,16]{1,0:T(8,128)S(1)} %multiply_reduce_fusion.2), channel_id=1, replica_groups=mesh['section'=8,'row'=16,'col'=4] {'col'}, use_global_device_ids=true, to_apply=%region_3.0 | all-reduce | flops 256 | bytes 2048 | tf_op jit(solution)/shard_map/psum | solution.py:61
  96.0 11.1 %all_gather.14 = bf16[256,1024]{1,0:T(8,128)(2,1)S(1)} all-gather(bf16[256,256]{1,0:T(8,128)(2,1)S(1)} %bitcast.65), channel_id=1, replica_groups=mesh['section'=8,'row'=16,'col'=4] {'col'}, dimensions={1}, use_global_device_ids=true | all-gather | bytes 655360 | tf_op jit(solution)/shard_map/all_gather | solution.py:65
  107.1 5.2 %fusion.3 = (bf16[256,1024]{1,0:T(8,128)(2,1)}, f32[256,1024]{1,0:T(8,128)S(1)}) fusion(bf16[256,1024]{1,0:T(8,128)(2,1)S(1)} %all_gather.14, bf16[1024,1024]{1,0:T(8,128)(2,1)} %all-gather.4.cloned.1.call-done), kind=kOutput, calls=%fused_computation.8 | convolution fusion | flops 553910272 | bytes 4194304 | tf_op jit(solution)/shard_map/dot_general | solution.py:67
  112.4 24.8 %reduce-scatter.3.cloned.1.call-done = bf16[256,1024]{1,0:T(8,128)(2,1)} async-done(((bf16[256,4096]{1,0:T(8,128)(2,1)}), bf16[256,1024]{1,0:T(8,128)(2,1)}) %reduce-scatter.3.cloned.1.call-update) | async-done | bytes 524304 | tf_op jit(solution)/shard_map/reduce_scatter | solution.py:82
  137.1 3.6 %convolution_convert_fusion.1 = bf16[256,1024]{1,0:T(8,128)(2,1)} fusion(bf16[1024,1024]{1,0:T(8,128)(2,1)} %all-gather.4.cloned.1.call-done, f32[256,1024]{1,0:T(8,128)S(1)} %get-tuple-element.64, bf16[256,1024]{1,0:T(8,128)(2,1)} %reduce-scatter.3.cloned.1.call-done), kind=kOutput, calls=%fused_computation.3 | convolution fusion | flops 540016640 | bytes 4194304 | tf_op jit(solution)/shard_map/dot_general | solution.py:47
  141.3 24.0 %reduce-scatter.5.cloned.1.call-done = bf16[256,256]{1,0:T(8,128)(2,1)} async-done(((bf16[256,1024]{1,0:T(8,128)(2,1)}), bf16[256,256]{1,0:T(8,128)(2,1)}) %reduce-scatter.5.cloned.1.call-update) | async-done | bytes 131088 | tf_op jit(solution)/shard_map/reduce_scatter | solution.py:87
  167.6 11.5 %all-reduce = (f32[16,16]{1,0:T(8,128)S(1)}, f32[16,16]{1,0:T(8,128)S(1)}) all-reduce(f32[16,16]{1,0:T(8,128)S(1)} %multiply_reduce_fusion, f32[16,16]{1,0:T(8,128)S(1)} %reduce_sum.41), channel_id=1, replica_groups=mesh['section'=8,'row'=16,'col'=4] {'col'}, use_global_device_ids=true, to_apply=%region_9.0 | all-reduce | flops 512 | bytes 4096 | tf_op jit(solution)/shard_map/psum | solution.py:91
  179.1 1.1 multiply_convert_fusion
  180.3 1.3 collective-permute-start.5
  181.6 4.1 %collective-permute-start.4 = (bf16[3,16,256]{2,1,0:T(8,128)(2,1)S(1)}, bf16[3,16,256]{2,1,0:T(8,128)(2,1)S(1)}, u32[]{:S(2)}, u32[]{:S(2)}) collective-permute-start(bf16[3,16,256]{2,1,0:T(8,128)(2,1)S(1)} %get-tuple-element.10), channel_id=1, source_target_pairs={{0,64},{64,128},{128,192},{192,256},{256,320},{320,384},{384,448},... | collective-permute-start | bytes 73736 | tf_op jit(solution)/shard_map/ppermute | solution.py:19
  186.6 9.8 %collective-permute-start.7 = (bf16[22,3,256]{2,1,0:T(4,128)(2,1)S(1)}, bf16[22,3,256]{2,1,0:T(4,128)(2,1)S(1)}, u32[]{:S(2)}, u32[]{:S(2)}) collective-permute-start(bf16[22,3,256]{2,1,0:T(4,128)(2,1)S(1)} %get-tuple-element.7), channel_id=1, source_target_pairs={{4,0},{8,4},{12,8},{16,12},{20,16},{24,20},{28,24},{32,28},{36,32}... | collective-permute-start | bytes 101384 | tf_op jit(solution)/shard_map/ppermute | solution.py:22
  196.4 2.5 %collective-permute-start.6 = (bf16[22,3,256]{2,1,0:T(4,128)(2,1)S(1)}, bf16[22,3,256]{2,1,0:T(4,128)(2,1)S(1)}, u32[]{:S(2)}, u32[]{:S(2)}) collective-permute-start(bf16[22,3,256]{2,1,0:T(4,128)(2,1)S(1)} %get-tuple-element.6), channel_id=1, source_target_pairs={{0,4},{4,8},{8,12},{12,16},{16,20},{20,24},{24,28},{28,32},{32,36}... | collective-permute-start | bytes 101384 | tf_op jit(solution)/shard_map/ppermute | solution.py:19
  198.9 6.5 %all-gather.6.cloned.1.call-done = bf16[256,4096]{1,0:T(8,128)(2,1)} async-done(((bf16[256,1024]{1,0:T(8,128)(2,1)}), bf16[256,4096]{1,0:T(8,128)(2,1)}) %all-gather.6.cloned.1.call-update) | async-done | bytes 2097168 | tf_op jit(solution)/shard_map/all_gather | solution.py:71
  205.4 3.0 %fusion = bf16[256,256]{1,0:T(8,128)(2,1)} fusion(bf16[256,4096]{1,0:T(8,128)(2,1)} %all-gather.6.cloned.1.call-done, bf16[4096,256]{1,0:T(8,128)(2,1)S(1)} %copy-done, bf16[256,256]{1,0:T(8,128)(2,1)S(1)} %bitcast.66), kind=kOutput, calls=%fused_computation.5 | convolution fusion | flops 537067520 | bytes 4456448 | tf_op jit(solution)/shard_map/dot_general | solution.py:73
  208.5 2.4 %fusion.24 = f32[16,16,256]{2,1,0:T(8,128)} fusion(f32[22,22,256]{2,1,0:T(8,128)S(1)} %maximum_convert_fusion.1, bf16[16,16,256]{2,1,0:T(8,128)(2,1)S(1)} %copy-done.1, f32[256]{0:T(256)S(1)} %bitcast.162, f32[256]{0:T(256)S(1)} %bitcast.164, f32[256]{0:T(256)S(1)} %bitcast.70, f32[256]{0:T(256)S(1)} %bitcast.72, f32[256]{0:T(256)S(1)} %bitcast.74, ...), kind=kLoop, calls=%fused_computation.39 | loop fusion | flops 6488064 | bytes 13288448 | tf_op jit(solution)/shard_map/add | solution.py:102
  (49 shorter events, 8.0 us)
Async XLA Ops:
  7.2 50.6 %all-gather.8.cloned.1.call-start = ((), (), s32[]{:S(2)}) async-start(), calls=%async_computation.4 | async-start | bytes 2228224 | tf_op jit(solution)/shard_map/all_gather | solution.py:75
  7.9 99.2 %all-gather.4.cloned.1.call-start = ((), (), s32[]{:S(2)}) async-start(), calls=%async_computation.2 | async-start | bytes 2228224 | tf_op jit(solution)/shard_map/all_gather | solution.py:68
  8.6 128.5 %reduce-scatter.3.cloned.1.call-start = ((), (), s32[]{:S(2)}) async-start(), calls=%async_computation.5 | async-start | bytes 2621440 | tf_op jit(solution)/shard_map/reduce_scatter | solution.py:82
  61.5 0.9 copy-start.2
  61.5 5.5 %copy-start.3 = (f32[7,7,256]{2,1,0:T(8,128)S(1)}, f32[7,7,256]{2,1,0:T(8,128)}, u32[]{:S(2)}) copy-start(f32[7,7,256]{2,1,0:T(8,128)} %param.7) | copy-start | bytes 150532
  61.5 103.8 %reduce-scatter.5.cloned.1.call-start = ((), (), s32[]{:S(2)}) async-start(), calls=%async_computation.6 | async-start | bytes 655360 | tf_op jit(solution)/shard_map/reduce_scatter | solution.py:87
  62.4 4.6 %collective-permute-start = (bf16[3,16,256]{2,1,0:T(8,128)(2,1)S(1)}, bf16[3,16,256]{2,1,0:T(8,128)(2,1)S(1)}, u32[]{:S(2)}, u32[]{:S(2)}) collective-permute-start(bf16[3,16,256]{2,1,0:T(8,128)(2,1)S(1)} %get-tuple-element.13), channel_id=1, source_target_pairs={{0,64},{64,128},{128,192},{192,256},{256,320},{320,384},{384,448},... | collective-permute-start | bytes 73736 | tf_op jit(solution)/shard_map/ppermute | solution.py:19
  65.7 4.6 %collective-permute-start.1 = (bf16[3,16,256]{2,1,0:T(8,128)(2,1)S(1)}, bf16[3,16,256]{2,1,0:T(8,128)(2,1)S(1)}, u32[]{:S(2)}, u32[]{:S(2)}) collective-permute-start(bf16[3,16,256]{2,1,0:T(8,128)(2,1)S(1)} %get-tuple-element.12), channel_id=1, source_target_pairs={{64,0},{128,64},{192,128},{256,192},{320,256},{384,320},{448,384},... | collective-permute-start | bytes 73736 | tf_op jit(solution)/shard_map/ppermute | solution.py:22
  70.3 6.5 %collective-permute-start.3 = (bf16[22,3,256]{2,1,0:T(4,128)(2,1)S(1)}, bf16[22,3,256]{2,1,0:T(4,128)(2,1)S(1)}, u32[]{:S(2)}, u32[]{:S(2)}) collective-permute-start(bf16[22,3,256]{2,1,0:T(4,128)(2,1)S(1)} %get-tuple-element.9), channel_id=1, source_target_pairs={{4,0},{8,4},{12,8},{16,12},{20,16},{24,20},{28,24},{32,28},{36,32}... | collective-permute-start | bytes 101384 | tf_op jit(solution)/shard_map/ppermute | solution.py:22
  73.9 3.8 %collective-permute-start.2 = (bf16[22,3,256]{2,1,0:T(4,128)(2,1)S(1)}, bf16[22,3,256]{2,1,0:T(4,128)(2,1)S(1)}, u32[]{:S(2)}, u32[]{:S(2)}) collective-permute-start(bf16[22,3,256]{2,1,0:T(4,128)(2,1)S(1)} %get-tuple-element.8), channel_id=1, source_target_pairs={{0,4},{4,8},{8,12},{12,16},{16,20},{20,24},{24,28},{28,32},{32,36}... | collective-permute-start | bytes 101384 | tf_op jit(solution)/shard_map/ppermute | solution.py:19
  77.8 18.1 %copy-start.4 = (f32[256]{0:T(256)S(1)}, f32[256]{0:T(256)}, u32[]{:S(2)}) copy-start(f32[256]{0:T(256)} %param.8) | copy-start | bytes 3076
  140.7 64.7 %copy-start = (bf16[4096,256]{1,0:T(8,128)(2,1)S(1)}, bf16[4096,256]{1,0:T(8,128)(2,1)}, u32[]{:S(2)}) copy-start(bf16[4096,256]{1,0:T(8,128)(2,1)} %all-gather.8.cloned.1.call-done) | copy-start | bytes 6291460
  140.7 64.7 %all-gather.6.cloned.1.call-start = ((), (), s32[]{:S(2)}) async-start(), calls=%async_computation.3 | async-start | bytes 2621440 | tf_op jit(solution)/shard_map/all_gather | solution.py:71
  180.3 5.4 %collective-permute-start.5 = (bf16[3,16,256]{2,1,0:T(8,128)(2,1)S(1)}, bf16[3,16,256]{2,1,0:T(8,128)(2,1)S(1)}, u32[]{:S(2)}, u32[]{:S(2)}) collective-permute-start(bf16[3,16,256]{2,1,0:T(8,128)(2,1)S(1)} %get-tuple-element.11), channel_id=1, source_target_pairs={{64,0},{128,64},{192,128},{256,192},{320,256},{384,320},{448,384},... | collective-permute-start | bytes 73736 | tf_op jit(solution)/shard_map/ppermute | solution.py:22
  181.6 5.0 %collective-permute-start.4 = (bf16[3,16,256]{2,1,0:T(8,128)(2,1)S(1)}, bf16[3,16,256]{2,1,0:T(8,128)(2,1)S(1)}, u32[]{:S(2)}, u32[]{:S(2)}) collective-permute-start(bf16[3,16,256]{2,1,0:T(8,128)(2,1)S(1)} %get-tuple-element.10), channel_id=1, source_target_pairs={{0,64},{64,128},{128,192},{192,256},{256,320},{320,384},{384,448},... | collective-permute-start | bytes 73736 | tf_op jit(solution)/shard_map/ppermute | solution.py:19
  186.6 21.8 %collective-permute-start.7 = (bf16[22,3,256]{2,1,0:T(4,128)(2,1)S(1)}, bf16[22,3,256]{2,1,0:T(4,128)(2,1)S(1)}, u32[]{:S(2)}, u32[]{:S(2)}) collective-permute-start(bf16[22,3,256]{2,1,0:T(4,128)(2,1)S(1)} %get-tuple-element.7), channel_id=1, source_target_pairs={{4,0},{8,4},{12,8},{16,12},{20,16},{24,20},{28,24},{32,28},{36,32}... | collective-permute-start | bytes 101384 | tf_op jit(solution)/shard_map/ppermute | solution.py:22
  196.4 12.0 %collective-permute-start.6 = (bf16[22,3,256]{2,1,0:T(4,128)(2,1)S(1)}, bf16[22,3,256]{2,1,0:T(4,128)(2,1)S(1)}, u32[]{:S(2)}, u32[]{:S(2)}) collective-permute-start(bf16[22,3,256]{2,1,0:T(4,128)(2,1)S(1)} %get-tuple-element.6), channel_id=1, source_target_pairs={{0,4},{4,8},{8,12},{12,16},{16,20},{20,24},{24,28},{28,32},{32,36}... | collective-permute-start | bytes 101384 | tf_op jit(solution)/shard_map/ppermute | solution.py:19
  205.4 3.2 %copy-start.1 = (bf16[16,16,256]{2,1,0:T(8,128)(2,1)S(1)}, bf16[16,16,256]{2,1,0:T(8,128)(2,1)}, u32[]{:S(2)}) copy-start(bf16[16,16,256]{2,1,0:T(8,128)(2,1)} %param.11) | copy-start | bytes 393220
Sparse Core Ops, SparseCore 0:
  10.1 47.6 all-gather.7
  59.9 40.5 all-gather.3
  103.3 33.7 reduce-scatter.2
  140.8 24.4 reduce-scatter.4
  167.3 38.0 all-gather.5
where the time goes:
time: 218 us; the launch traced here: 217 us
  waiting for transfers between devices  111 us (51%)
  blocking collectives  38.7 us (18%)
  starting transfers between devices  28.7 us (13%)
  matrix products  15.6 us (7%)
  between operations  14 us (6%)
  other arithmetic  8.02 us (4%)
    all_gather x1, waiting for transfers between devices, local(): lax.all_gather(w_out, 'row', axis=0, tiled=True)  49.1 us
    reduce_scatter x1, waiting for transfers between devices, local(): lax.psum_scatter(hidden_terms.astype(jnp.bfloat16), 'col', scatter_dimens...  24.8 us
    reduce_scatter x1, waiting for transfers between devices, local(): lax.psum_scatter(feature_terms.astype(jnp.bfloat16), 'col', scatter_dimen...  24 us
    ppermute x4, starting transfers between devices, extended(): lax.ppermute(lax.slice_in_dim(block, 0, width, axis=dim), axis, backward)  16 us
    ppermute x4, starting transfers between devices, extended(): lax.ppermute(lax.slice_in_dim(block, block.shape[dim] - width, None, axis...  12.5 us
    psum x1, blocking collectives, local(): lax.psum((jnp.sum(normed_grad, axis=-1), jnp.sum(normed_grad * normed, ax...  11.5 us
    all_gather x1, blocking collectives, local(): features = lax.all_gather(scaled, 'col', axis=1, tiled=True)  11.1 us
    psum x1, blocking collectives, local(): centre = lax.psum(jnp.sum(mixed, axis=-1), 'col')[..., None] / channels_all  9.2 us
  transfers between devices with their start and end apart: 13, of which 8 were waited for; matrix products, arithmetic and copies ran while one was open for 8% of the time, Pallas kernels for 0%

commit v1 on v0

v1 whole, which is shorter than its diff:
```python
import functools
import math

import jax
import jax.numpy as jnp
from jax import lax
from jax.experimental import pallas as pl
from jax.experimental.pallas import tpu as pltpu
from jax.sharding import PartitionSpec as P

KERNEL = 7
EPSILON = 1e-06
MESH = pl.DeviceIdType.MESH
F32, BF16 = jnp.float32, jnp.bfloat16
EDGE = 8


def dot_nn(left, right):
    return lax.dot_general(left, right, (((1,), (0,)), ((), ())), preferred_element_type=F32)


def dot_nt(left, right):
    return lax.dot_general(left, right, (((1,), (1,)), ((), ())), preferred_element_type=F32)


def body(
    image, kern, gain, w_in, w_out, up, out, igrad,
    hlon, hlat, hcor, pad, mix, feat, stat, stat2, ups, win, sl, wo, pre, gws, hb, ag,
    sums, fgs, fgr, fgo, obs, obr, obo, mgb, dinv,
    s_halo, r_halo, s_ft, r_ft, s_st, r_st, s_up, r_up, s_wl, s_ws, s_wp, r_w,
    s_sl, r_sl, s_wx, r_wx, s_zl, s_zs, s_zp, r_z, s_fg, r_fg, s_s2, r_s2, s_ob, r_ob, s_loc,
):
    nz, nr, nx = lax.axis_size("section"), lax.axis_size("row"), lax.axis_size("col")
    ny = nr // 2
    long, short = ny // 2, ny - 1 - ny // 2
    zlong, zshort = nz // 2, nz - 1 - nz // 2
    z, r, x = lax.axis_index("section"), lax.axis_index("row"), lax.axis_index("col")
    y, c = lax.div(r, 2), lax.rem(r, 2)
    turn = 1 - 2 * c
    cells = 256

    def at_y(d):
        return lax.rem(y + d + ny, ny)

    def at_z(d):
        return lax.rem(z + d + nz, nz)

    def at_x(d):
        return lax.rem(x + d, nx)

    def row_dev(yy, cc):
        return {"row": 2 * yy + cc}

    partner = row_dev(y, 1 - c)

    def send(src, dst, ssem, rsem, dev):
        return pltpu.make_async_remote_copy(
            src_ref=src, dst_ref=dst, send_sem=ssem, recv_sem=rsem, device_id=dev,
            device_id_type=MESH,
        )

    def got(ref, rsem):
        send(ref, ref, s_loc.at[0], rsem, partner).wait_recv()

    around = [(dz, dr) for dz in (-1, 0, 1) for dr in (-1, 0, 1) if (dz, dr) != (0, 0)]

    stat[...] = jnp.zeros(stat.shape, F32)
    stat2[...] = jnp.zeros(stat2.shape, F32)

    barrier = pltpu.get_barrier_semaphore()
    greeted = 0
    for dz, dr in around:
        pl.semaphore_signal(
            barrier, inc=1, device_id={"section": at_z(dz), "row": lax.rem(r + dr + nr, nr)},
            device_id_type=MESH,
        )
        greeted += 1
    for d in range(1, nx):
        pl.semaphore_signal(barrier, inc=1, device_id={"col": at_x(d)}, device_id_type=MESH)
        greeted += 1
    for d in range(1, ny):
        pl.semaphore_signal(barrier, inc=1, device_id=row_dev(at_y(d), c), device_id_type=MESH)
        greeted += 1
    for d in (-1, 1):
        pl.semaphore_signal(barrier, inc=1, device_id={"section": at_z(d)}, device_id_type=MESH)
        greeted += 1
    pl.semaphore_signal(barrier, inc=1, device_id=partner, device_id_type=MESH)
    greeted += 1
    pl.semaphore_wait(barrier, greeted)

    def lat_of(dz, ref_lats):
        return pl.ds(ref_lats - 3, 3) if dz > 0 else pl.ds(0, 3)

    def lon_of(dr):
        return pl.ds(16 - EDGE, EDGE) if dr > 0 else pl.ds(0, EDGE)

    def halo_slot(p, dz, dr):
        if dz == 0:
            return hlon.at[p, 0 if dr > 0 else 1]
        if dr == 0:
            return hlat.at[p, 0 if dz > 0 else 1]
        return hcor.at[p, (0 if dz > 0 else 2) + (0 if dr > 0 else 1)]

    def inside(dz, dr):
        zz, rr = z + dz, r + dr
        return jnp.logical_and(
            jnp.logical_and(zz >= 0, zz < nz), jnp.logical_and(rr >= 0, rr < nr)
        )

    def halo_copy(p, n, ref):
        dz, dr = around[n]
        if dz == 0:
            src = ref.at[:, lon_of(dr), :]
        elif dr == 0:
            src = ref.at[lat_of(dz, 16)]
        else:
            src = ref.at[lat_of(dz, 16), lon_of(dr), :]
        dev = {"section": at_z(dz), "row": lax.rem(r + dr + nr, nr)}
        return send(src, halo_slot(p, dz, dr), s_halo.at[p, n], r_halo.at[p, n], dev)

    def halo_start(p, ref):
        for n, (dz, dr) in enumerate(around):
            @pl.when(inside(dz, dr))
            def _():
                halo_copy(p, n, ref).start()

    def halo_sent(p, ref):
        for n, (dz, dr) in enumerate(around):
            @pl.when(inside(dz, dr))
            def _():
                halo_copy(p, n, ref).wait_send()

    def halo_take(p):
        for n, (dz, dr) in enumerate(around):
            lats = pl.ds(3, 16) if dz == 0 else (pl.ds(0, 3) if dz > 0 else pl.ds(19, 3))
            lons = pl.ds(8, 16) if dr == 0 else (pl.ds(0, 8) if dr > 0 else pl.ds(24, 8))
            slot = halo_slot(p, dz, dr)
            shape = (16 if dz == 0 else 3, 16 if dr == 0 else 8, 256)

            @pl.when(inside(-dz, -dr))
            def _():
                got(slot, r_halo.at[p, n])
                pad[lats, lons, :] = slot[...].astype(F32)

            @pl.when(jnp.logical_not(inside(-dz, -dr)))
            def _():
                pad[lats, lons, :] = jnp.zeros(shape, F32)

    def conv(flip, emit):
        def group(g, carry):
            i0 = g * 4
            acc = [jnp.zeros((16, 256), F32) for _ in range(4)]
            for b in range(KERNEL):
                rows = [pad[i0 + t, pl.ds(5 + b, 16), :] for t in range(10)]
                for a in range(KERNEL):
                    tap = kern[KERNEL - 1 - a, KERNEL - 1 - b, :] if flip else kern[a, b, :]
                    tap = tap.reshape(1, 256)
                    for q in range(4):
                        acc[q] = acc[q] + rows[q + a] * tap
            for q in range(4):
                emit(i0 + q, acc[q])
            return carry

        lax.fori_loop(0, 4, group, 0)

    def win_send(far, t):
        owner = at_y(-turn * t) if far else at_y(turn * t)
        dev = row_dev(at_y(turn) if far else at_y(-turn), c)
        slot = 2 * owner + c
        src = w_in if t == 0 else win.at[slot]
        return send(src, win.at[slot], (s_wl if far else s_ws).at[t], r_w.at[slot], dev)

    def win_share(t, owner):
        slot = 2 * owner + c
        src = w_in if t == 0 else win.at[slot]
        return send(src, win.at[slot], s_wp.at[t], r_w.at[slot], partner)

    def win_relay(d):
        if d <= long:
            owner = at_y(-turn * d)
            got(win.at[2 * owner + c], r_w.at[2 * owner + c])
            if d < long:
                win_send(True, d).start()
            win_share(d, owner).start()
        if d <= short:
            owner = at_y(turn * d)
            got(win.at[2 * owner + c], r_w.at[2 * owner + c])
            if d < short:
                win_send(False, d).start()
            win_share(long + d, owner).start()

    def zone(zz, cc):
        return wo.at[:, :, cc, zz]

    def wo_send(far, t):
        owner = at_z(-turn * t) if far else at_z(turn * t)
        dev = {"section": at_z(turn) if far else at_z(-turn)}
        ref = zone(owner, c)
        return send(ref, ref, (s_zl if far else s_zs).at[t], r_z.at[2 * owner + c], dev)

    def wo_share(t, owner):
        ref = zone(owner, c)
        return send(ref, ref, s_zp.at[t], r_z.at[2 * owner + c], partner)

    def wo_relay(d):
        if d <= zlong:
            owner = at_z(-turn * d)
            got(zone(owner, c), r_z.at[2 * owner + c])
            if d < zlong:
                wo_send(True, d).start()
            wo_share(d, owner).start()
        if d <= zshort:
            owner = at_z(turn * d)
            got(zone(owner, c), r_z.at[2 * owner + c])
            if d < zshort:
                wo_send(False, d).start()
            wo_share(zlong + d, owner).start()

    halo_start(0, image)
    win_send(True, 0).start()
    win_send(False, 0).start()
    win_share(0, y).start()

    my_rows = w_out.at[pl.ds(pl.multiple_of(z * 32, 32), 32), :]

    def slice_send(d):
        return send(my_rows, sl.at[y], s_sl.at[d - 1], r_sl.at[y], row_dev(at_y(d), c))

    def to_col(src, dst, ssem, rsem, d):
        return send(src, dst, ssem.at[d - 1], rsem.at[x], {"col": at_x(d)})

    for d in range(1, ny):
        slice_send(d).start()
    for d in range(1, nx):
        to_col(up, ups.at[x], s_up, r_up, d).start()
    local = [
        pltpu.make_async_copy(w_in, win.at[r], s_loc.at[1]),
        pltpu.make_async_copy(my_rows, sl.at[y], s_loc.at[2]),
        pltpu.make_async_copy(up, ups.at[x], s_loc.at[3]),
    ]
    for copy in local:
        copy.start()

    pad[pl.ds(3, 16), pl.ds(8, 16), :] = image[...].astype(F32)
    halo_take(0)
    win_relay(1)

    def keep(i, value):
        mix[i] = value

    conv(False, keep)

    flat = mix[...].reshape(cells, 256)
    mean_own = jnp.sum(flat, axis=-1, keepdims=True) * (1.0 / 256)
    centred = flat - mean_own
    square = jnp.sum(centred * centred, axis=-1, keepdims=True)
    g_row = gain[...]
    feat[x, pl.ds(0, cells), :] = (centred * g_row).astype(BF16)
    g_high = g_row.astype(BF16).astype(F32)
    tail = lax.broadcasted_iota(jnp.int32, (16, 256), 0)
    feat[x, pl.ds(cells, 16), :] = jnp.where(
        tail == 0, g_high, jnp.where(tail == 1, g_row - g_high, 0.0)
    ).astype(BF16)
    lane = lax.broadcasted_iota(jnp.int32, (cells, 128), 1)

    def as_rows(first, second):
        both = jnp.where(lane == 0, first, jnp.where(lane == 1, second, 0.0))
        return both.T[0:8, :]

    rows_own = as_rows(mean_own, square)
    s_rows = rows_own
    stat_own = pl.ds(pl.multiple_of(x * 8, 8), 8)
    stat[stat_own, :] = s_rows
    for d in range(1, nx):
        to_col(stat.at[stat_own, :], stat.at[stat_own, :], s_st, r_st, d).start()
        to_col(feat.at[x], feat.at[x], s_ft, r_ft, d).start()

    for copy in local:
        copy.wait()
    for d in range(1, ny):
        got(sl.at[at_y(d)], r_sl.at[at_y(d)])

    def cross(d):
        dest = at_x(d)
        return send(
            sl.at[pl.ds(2 * dest, 2)], wo.at[x, :, c, z], s_wx.at[d - 1], r_wx.at[x],
            {"col": dest},
        )

    for d in range(1, nx):
        cross(d).start()
    mine = pltpu.make_async_copy(sl.at[pl.ds(2 * x, 2)], wo.at[x, :, c, z], s_loc.at[4])
    mine.start()
    win_relay(2)
    mine.wait()
    for d in range(1, nx):
        got(wo.at[at_x(d), :, c, z], r_wx.at[at_x(d)])
    wo_send(True, 0).start()
    wo_send(False, 0).start()
    wo_share(0, z).start()
    for d in range(3, long + 1):
        win_relay(d)

    for d in range(1, nx):
        k = at_x(d)
        got(stat.at[pl.ds(pl.multiple_of(k * 8, 8), 8), :], r_st.at[k])
        got(feat.at[k], r_ft.at[k])
    wo_relay(1)
    for yy in range(ny):
        slot = 2 * yy + 1 - c
        got(win.at[slot], r_w.at[slot])

    columns = stat[...].T
    means = [columns[:, 8 * k : 8 * k + 1] for k in range(nx)]
    centre = (means[0] + means[1] + means[2] + means[3]) * 0.25
    shifts = [m - centre for m in means]
    total = columns[:, 1:2] + columns[:, 9:10] + columns[:, 17:18] + columns[:, 25:26]
    spread = total + 256.0 * (
        shifts[0] * shifts[0] + shifts[1] * shifts[1] + shifts[2] * shifts[2]
        + shifts[3] * shifts[3]
    )
    inv_std = lax.rsqrt(spread * (1.0 / 1024) + EPSILON)
    for k in range(nx):
        dinv[k] = jnp.broadcast_to(shifts[k] * inv_std, (cells, 128))
    dinv[4] = jnp.broadcast_to(inv_std, (cells, 128))
    dinv[5] = jnp.broadcast_to(centre, (cells, 128))

    def wide(n):
        half = dinv[n]
        return jnp.concatenate([half, half], axis=1)

    def first_product(n, carry):
        cols = pl.ds(pl.multiple_of(n * 256, 256), 256)
        acc = jnp.zeros((cells, 256), F32)
        shift = jnp.zeros((cells, 256), F32)
        gsum = jnp.zeros((1, 256), F32)
        for k in range(nx):
            block = win[4 * k : 4 * k + 4, :, cols].reshape(256, 256)
            part = dot_nn(feat[k], block)
            acc = acc + part[:cells]
            row = part[cells : cells + 1] + part[cells + 1 : cells + 2]
            shift = shift + wide(k) * row
            gsum = gsum + row
        pre[:, cols] = acc * wide(4) + shift
        gws[:, cols] = jnp.broadcast_to(gsum, (8, 256))
        return carry

    lax.fori_loop(0, 4, first_product, 0)

    for d in range(2, zlong + 1):
        wo_relay(d)
    for d in range(1, nx):
        got(ups.at[at_x(d)], r_up.at[at_x(d)])
    for zz in range(nz):
        got(zone(zz, 1 - c), r_z.at[2 * zz + 1 - c])

    sums[...] = jnp.zeros(sums.shape, F32)

    def activation(n, carry):
        cols = pl.ds(pl.multiple_of(n * 256, 256), 256)
        grad = jnp.zeros((cells, 256), F32)
        for k in range(nx):
            block = wo[k, lax.div(n, 2), lax.rem(n, 2)].reshape(256, 256)
            grad = grad + dot_nt(ups[k].reshape(cells, 256), block)
        value = pre[:, cols]
        phi = 0.5 * (1.0 + lax.erf(value * (1.0 / math.sqrt(2.0))))
        slope = phi + value * jnp.exp(-0.5 * value * value) * (1.0 / math.sqrt(2.0 * math.pi))
        hb[:, cols] = (value * phi).astype(BF16)
        act = (grad * slope).astype(BF16)
        ag[:, cols] = act
        actf = act.astype(F32)
        one = actf * gws[0:1, cols]
        two = actf * value
        sums[0] += one[:, :128] + one[:, 128:]
        sums[1] += two[:, :128] + two[:, 128:]
        return carry

    lax.fori_loop(0, 4, activation, 0)

    def win_block(k):
        return win[pl.ds(pl.multiple_of(k * 4, 4), 4)].reshape(256, 1024)

    stat2[stat_own, :] = as_rows(
        jnp.sum(sums[0], axis=-1, keepdims=True), jnp.sum(sums[1], axis=-1, keepdims=True)
    )
    for d in range(1, nx):
        to_col(stat2.at[stat_own, :], stat2.at[stat_own, :], s_s2, r_s2, d).start()

    def fg_copy(d):
        return to_col(fgs.at[d - 1], fgr.at[x], s_fg, r_fg, d)

    def ob_copy(d):
        return to_col(obs.at[d - 1], obr.at[x], s_ob, r_ob, d)

    for d in (2, 1, 3):
        fgs[d - 1] = dot_nt(ag[...], win_block(at_x(d))).astype(BF16)
        fg_copy(d).start()
    fgo[...] = dot_nt(ag[...], win_block(x))
    for d in (2, 1, 3):
        obs[d - 1] = dot_nn(hb[...], wo[at_x(d)].reshape(1024, 256)).astype(BF16)
        ob_copy(d).start()
    obo[...] = dot_nn(hb[...], wo[x].reshape(1024, 256))

    for d in range(1, nx):
        k = at_x(d)
        got(stat2.at[pl.ds(pl.multiple_of(k * 8, 8), 8), :], r_s2.at[k])
        got(fgr.at[k], r_fg.at[k])
    feature = fgo[...]
    for d in range(1, nx):
        feature = feature + fgr[at_x(d)].astype(F32)
    columns2 = stat2[...].T
    first = (
        columns2[:, 0:1] + columns2[:, 8:9] + columns2[:, 16:17] + columns2[:, 24:25]
    ) * (1.0 / 1024)
    second = (
        columns2[:, 1:2] + columns2[:, 9:10] + columns2[:, 17:18] + columns2[:, 25:26]
    ) * (1.0 / 1024)
    inv_wide = wide(4)
    normed = (mix[...].reshape(cells, 256) - wide(5)) * inv_wide
    mixed_grad = inv_wide * (feature * g_row - first - normed * second)
    mgb[...] = mixed_grad.astype(BF16).reshape(16, 16, 256)
    halo_start(1, mgb)
    pad[pl.ds(3, 16), pl.ds(8, 16), :] = mixed_grad.reshape(16, 16, 256)

    for d in range(1, nx):
        got(obr.at[at_x(d)], r_ob.at[at_x(d)])
    branch = obo[...]
    for d in range(1, nx):
        branch = branch + obr[at_x(d)].astype(F32)
    out[...] = (image[...].astype(F32) + branch.reshape(16, 16, 256)).astype(BF16)

    halo_take(1)

    def finish(i, value):
        igrad[i] = up[i].astype(F32) + value

    conv(True, finish)

    halo_sent(0, image)
    halo_sent(1, mgb)
    for t in range(long):
        win_send(True, t).wait_send()
    for t in range(short):
        win_send(False, t).wait_send()
    for t in range(ny):
        win_share(t, y).wait_send()
    for t in range(zlong):
        wo_send(True, t).wait_send()
    for t in range(zshort):
        wo_send(False, t).wait_send()
    for t in range(nz):
        wo_share(t, z).wait_send()
    for d in range(1, ny):
        slice_send(d).wait_send()
    for d in range(1, nx):
        to_col(up, ups.at[x], s_up, r_up, d).wait_send()
        to_col(stat.at[stat_own, :], stat.at[stat_own, :], s_st, r_st, d).wait_send()
        to_col(feat.at[x], feat.at[x], s_ft, r_ft, d).wait_send()
        to_col(stat2.at[stat_own, :], stat2.at[stat_own, :], s_s2, r_s2, d).wait_send()
        cross(d).wait_send()
        fg_copy(d).wait_send()
        ob_copy(d).wait_send()


def local(image, conv_kernel, norm_gain, w_in, w_out, upstream):
    nz, nr, nx = lax.axis_size("section"), lax.axis_size("row"), lax.axis_size("col")
    ny = nr // 2
    height, breadth, chan = image.shape
    cells = height * breadth
    vmem = pl.BlockSpec(memory_space=pltpu.VMEM)
    dma = pltpu.SemaphoreType.DMA
    scratch = [
        pltpu.VMEM((2, 2, 16, EDGE, chan), BF16),
        pltpu.VMEM((2, 2, 3, 16, chan), BF16),
        pltpu.VMEM((2, 4, 3, EDGE, chan), BF16),
        pltpu.VMEM((22, 32, chan), F32),
        pltpu.VMEM((height, breadth, chan), F32),
        pltpu.VMEM((nx, cells + 16, chan), BF16),
        pltpu.VMEM((128, cells), F32),
        pltpu.VMEM((128, cells), F32),
        pltpu.VMEM((nx, height, breadth, chan), BF16),
        pltpu.VMEM((nr, 64, 1024), BF16),
        pltpu.VMEM((ny, 32, chan), BF16),
        pltpu.VMEM((nx, 2, 2, nz, 32, chan), BF16),
        pltpu.VMEM((cells, 1024), F32),
        pltpu.VMEM((8, 1024), F32),
        pltpu.VMEM((cells, 1024), BF16),
        pltpu.VMEM((cells, 1024), BF16),
        pltpu.VMEM((2, cells, 128), F32),
        pltpu.VMEM((nx - 1, cells, chan), BF16),
        pltpu.VMEM((nx, cells, chan), BF16),
        pltpu.VMEM((cells, chan), F32),
        pltpu.VMEM((nx - 1, cells, chan), BF16),
        pltpu.VMEM((nx, cells, chan), BF16),
        pltpu.VMEM((cells, chan), F32),
        pltpu.VMEM((height, breadth, chan), BF16),
        pltpu.VMEM((6, cells, 128), F32),
        dma((2, 8)), dma((2, 8)),
        dma((nx - 1,)), dma((nx,)),
        dma((nx - 1,)), dma((nx,)),
        dma((nx - 1,)), dma((nx,)),
        dma((ny // 2,)), dma((ny // 2,)), dma((ny,)), dma((nr,)),
        dma((ny - 1,)), dma((ny,)),
        dma((nx - 1,)), dma((nx,)),
        dma((nz // 2,)), dma((nz // 2,)), dma((nz,)), dma((2 * nz,)),
        dma((nx - 1,)), dma((nx,)),
        dma((nx - 1,)), dma((nx,)),
        dma((nx - 1,)), dma((nx,)),
        dma((5,)),
    ]
    return pl.pallas_call(
        body,
        out_shape=(
            jax.ShapeDtypeStruct(image.shape, BF16),
            jax.ShapeDtypeStruct(image.shape, F32),
        ),
        in_specs=[vmem] * 6,
        out_specs=(vmem, vmem),
        scratch_shapes=scratch,
        compiler_params=pltpu.CompilerParams(
            collective_id=0, has_side_effects=True, vmem_limit_bytes=60 * 1024 * 1024
        ),
        name="block",
    )(image, conv_kernel, norm_gain.reshape(1, chan), w_in, w_out, upstream)


def solution(mesh):
    in_specs = (
        P("section", "row", "col"),
        P(None, None, "col"),
        P("col"),
        P("row", "col"),
        P("row", "col"),
        P("section", "row", "col"),
    )
    out_specs = (P("section", "row", "col"), P("section", "row", "col"))
    return jax.shard_map(local, mesh=mesh, in_specs=in_specs, out_specs=out_specs, check_vma=False)
```

time: 218 us -> 75.8 us (0.35)
  waiting for transfers between devices: 111 us -> 0 us
  Pallas kernels: 0 us -> 72.7 us
  blocking collectives: 38.7 us -> 0 us
  starting transfers between devices: 28.7 us -> 0 us
  matrix products: 15.6 us -> 0 us
  between operations: 14 us -> 0.65 us
  other arithmetic: 8.02 us -> 0 us
    pallas_call x0 -> x1, Pallas kernels: none -> 72.7 us  [local(): pl.pallas_call(body, out_shape=(jax.ShapeDtypeStruct(image.shape, BF16),...]
    all_gather x3 -> x0, waiting for transfers between devices: 55.6 us -> none  [the longest x1 49.1 us: local(): lax.all_gather(w_out, 'row', axis=0, tiled=True)]
    reduce_scatter x2 -> x0, waiting for transfers between devices: 48.8 us -> none  [the longest x1 24.8 us: local(): lax.psum_scatter(hidden_terms.astype(jnp.bfloat16), 'col', scatter_dimens...]
    ppermute x8 -> x0, starting transfers between devices: 28.5 us -> none  [the longest x4 16 us: extended(): lax.ppermute(lax.slice_in_dim(block, 0, width, axis=dim), axis, backward)]
    psum x3 -> x0, blocking collectives: 27.6 us -> none  [the longest x1 11.5 us: local(): lax.psum((jnp.sum(normed_grad, axis=-1), jnp.sum(normed_grad * normed, ax...]
    dot_general x4 -> x0, matrix products: 15.6 us -> none  [the longest x2 7.29 us: transposed(): lax.dot_general(left, right, (((1,), (1,)), ((), ())), preferred_element_...]
    all_gather x1 -> x0, blocking collectives: 11.1 us -> none  [local(): features = lax.all_gather(scaled, 'col', axis=1, tiled=True)]
    ppermute x8 -> x0, waiting for transfers between devices: 5.19 us -> none  [the longest x4 3.34 us: extended(): lax.ppermute(lax.slice_in_dim(block, 0, width, axis=dim), axis, backward)]
  transfers between devices with their start and end apart: 13 -> 0, of which waited for: 8 -> 0; matrix products, arithmetic and copies ran while one was open for 8% -> 0% of each run, Pallas kernels for 0% -> 0%
where the time goes in v1:
time: 75.8 us; the launch traced here: 75.6 us
  Pallas kernels  72.7 us (96%)
  local copies, waits for them, and re-layouts  2.32 us (3%)
    pallas_call x1, Pallas kernels, local(): pl.pallas_call(body, out_shape=(jax.ShapeDtypeStruct(image.shape, BF16),...  72.7 us
    unnamed x4, local copies, waits for them, and re-layouts  2.32 us

profile of v1, /device:TPU:1, one launch (start us, length us, event | category | flops | bytes accessed | tf_op | source)
XLA Modules:
  0.0 75.6 jit_solution(13224983184981431448)
XLA Ops:
  0.6 72.7 %block.1 = (bf16[16,16,256]{2,1,0:T(8,128)(2,1)}, f32[16,16,256]{2,1,0:T(8,128)}) custom-call(bf16[16,16,256]{2,1,0:T(8,128)(2,1)} %image.1, f32[7,7,256]{2,1,0:T(8,128)} %kern.1, f32[1,256]{1,0:T(1,128)} %bitcast.1, bf16[64,1024]{1,0:T(8,128)(2,1)} %w_in.1, bf16[256,256]{1,0:T(8,128)(2,1)} %w_out.1, bf16[16,16,256]{2,1,0:T(8,128)(2,1)} %up.1), custom_call_target="tpu_custom_call" | custom-call | tf_op jit(solution)/shard_map/block/pallas_call | solution.py:511
  73.3 0.0 copy-start
  73.3 1.6 %copy.10 = bf16[16,16,256]{2,1,0:T(8,128)(2,1)} copy(bf16[16,16,256]{2,1,0:T(8,128)(2,1)} %get-tuple-element.4) | data formatting | bytes 262144
  74.9 0.0 copy-done
  74.9 0.7 copy.11
Async XLA Ops:
  73.3 1.6 %copy-start = (f32[16,16,256]{2,1,0:T(8,128)S(1)}, f32[16,16,256]{2,1,0:T(8,128)}, u32[]{:S(2)}) copy-start(f32[16,16,256]{2,1,0:T(8,128)} %get-tuple-element.5) | copy-start | bytes 786436

commit v2 on v1

v2 whole, which is shorter than its diff:
```python
import functools
import math

import jax
import jax.numpy as jnp
from jax import lax
from jax.experimental import pallas as pl
from jax.experimental.pallas import tpu as pltpu
from jax.sharding import PartitionSpec as P

KERNEL = 7
EPSILON = 1e-06
MESH = pl.DeviceIdType.MESH
F32, BF16 = jnp.float32, jnp.bfloat16
EDGE = 8


def dot_nn(left, right):
    return lax.dot_general(left, right, (((1,), (0,)), ((), ())), preferred_element_type=F32)


def dot_nt(left, right):
    return lax.dot_general(left, right, (((1,), (1,)), ((), ())), preferred_element_type=F32)


def body(
    image_hbm, kern_hbm, gain_hbm, w_in, w_out, up_hbm, out, igrad,
    image, kern, gain,
    hlon, hlat, hcor, pad, mix, feat, stat, stat2, ups, win, sl, wo, pre, gws, hb, ag,
    sums, fg2, fgk, fgs, fge, fgr, fgo, ob2, obk, obs, obe, obr, obo, mgb, dinv,
    s_halo, r_halo, s_ft, r_ft, s_st, r_st, s_up, r_up, s_w, r_w, r_wp,
    s_sl, r_sl, s_wx, r_wx, s_z, r_z, r_zp, s_fg, r_fg, s_s2, r_s2, s_ob, r_ob, s_loc,
):
    nz, nr, nx = lax.axis_size("section"), lax.axis_size("row"), lax.axis_size("col")
    ny = nr // 2
    long, short = ny // 2, ny - 1 - ny // 2
    zlong, zshort = nz // 2, nz - 1 - nz // 2
    z, r, x = lax.axis_index("section"), lax.axis_index("row"), lax.axis_index("col")
    y, c = lax.div(r, 2), lax.rem(r, 2)
    turn = 1 - 2 * c
    cells, half = 256, 128

    def at_y(d):
        return lax.rem(y + d + ny, ny)

    def at_z(d):
        return lax.rem(z + d + nz, nz)

    def at_x(d):
        return lax.rem(x + d, nx)

    def row_dev(yy, cc):
        return {"row": 2 * yy + cc}

    partner = row_dev(y, 1 - c)

    def send(src, dst, ssem, rsem, dev):
        return pltpu.make_async_remote_copy(
            src_ref=src, dst_ref=dst, send_sem=ssem, recv_sem=rsem, device_id=dev,
            device_id_type=MESH,
        )

    def got(ref, rsem):
        send(ref, ref, s_loc.at[0], rsem, partner).wait_recv()

    def left_here(ref, ssem):
        send(ref, ref, ssem, s_loc.at[0], partner).wait_send()

    around = [(dz, dr) for dz in (-1, 0, 1) for dr in (-1, 0, 1) if (dz, dr) != (0, 0)]

    loads = [
        pltpu.make_async_copy(image_hbm, image, s_loc.at[5]),
        pltpu.make_async_copy(kern_hbm, kern, s_loc.at[6]),
        pltpu.make_async_copy(gain_hbm, gain, s_loc.at[7]),
    ]
    barrier = pltpu.get_barrier_semaphore()
    greeted = 0
    for dz, dr in around:
        pl.semaphore_signal(
            barrier, inc=1, device_id={"section": at_z(dz), "row": lax.rem(r + dr + nr, nr)},
            device_id_type=MESH,
        )
        greeted += 1
    for d in range(1, nx):
        pl.semaphore_signal(barrier, inc=1, device_id={"col": at_x(d)}, device_id_type=MESH)
        greeted += 1
    for d in range(1, ny):
        pl.semaphore_signal(barrier, inc=1, device_id=row_dev(at_y(d), c), device_id_type=MESH)
        greeted += 1
    for d in (-1, 1):
        pl.semaphore_signal(barrier, inc=1, device_id={"section": at_z(d)}, device_id_type=MESH)
        greeted += 1
    pl.semaphore_signal(barrier, inc=1, device_id=partner, device_id_type=MESH)
    greeted += 1
    for copy in loads:
        copy.start()
    stat[pl.ds(8 * nx, 128 - 8 * nx), :] = jnp.zeros((128 - 8 * nx, cells), F32)
    stat2[pl.ds(8 * nx, 128 - 8 * nx), :] = jnp.zeros((128 - 8 * nx, cells), F32)
    pl.semaphore_wait(barrier, greeted)

    def lat_of(dz, ref_lats):
        return pl.ds(ref_lats - 3, 3) if dz > 0 else pl.ds(0, 3)

    def lon_of(dr):
        return pl.ds(16 - EDGE, EDGE) if dr > 0 else pl.ds(0, EDGE)

    def halo_slot(p, dz, dr):
        if dz == 0:
            return hlon.at[p, 0 if dr > 0 else 1]
        if dr == 0:
            return hlat.at[p, 0 if dz > 0 else 1]
        return hcor.at[p, (0 if dz > 0 else 2) + (0 if dr > 0 else 1)]

    def inside(dz, dr):
        zz, rr = z + dz, r + dr
        return jnp.logical_and(
            jnp.logical_and(zz >= 0, zz < nz), jnp.logical_and(rr >= 0, rr < nr)
        )

    def halo_copy(p, n, ref):
        dz, dr = around[n]
        if dz == 0:
            src = ref.at[:, lon_of(dr), :]
        elif dr == 0:
            src = ref.at[lat_of(dz, 16)]
        else:
            src = ref.at[lat_of(dz, 16), lon_of(dr), :]
        dev = {"section": at_z(dz), "row": lax.rem(r + dr + nr, nr)}
        return send(src, halo_slot(p, dz, dr), s_halo.at[p], r_halo.at[p], dev)

    def halo_start(p, ref):
        for n in range(len(around)):
            halo_copy(p, n, ref).start()

    halo_bytes = win.at[pl.ds(0, 7), pl.ds(0, 16)]

    def fill(lats, lons, value):
        pad[0, lats, lons, :] = value[:, :, :128]
        pad[1, lats, lons, :] = value[:, :, 128:]

    def halo_take(p):
        got(halo_bytes, r_halo.at[p])
        for dz, dr in around:
            lats = pl.ds(3, 16) if dz == 0 else (pl.ds(0, 3) if dz > 0 else pl.ds(19, 3))
            lons = pl.ds(8, 16) if dr == 0 else (pl.ds(0, 8) if dr > 0 else pl.ds(24, 8))
            slot = halo_slot(p, dz, dr)
            value = slot[...].astype(F32)
            fill(lats, lons, jnp.where(inside(-dz, -dr), value, 0.0))

    def conv(flip, top, emit):
        def lanes(h, carry):
            cols = pl.ds(pl.multiple_of(h * 128, 128), 128)
            acc = [jnp.zeros((16, 128), F32) for _ in range(8)]
            for b in range(KERNEL):
                rows = [pad[h, top + t, pl.ds(5 + b, 16), :] for t in range(14)]
                for a in range(KERNEL):
                    at = (KERNEL - 1 - a, KERNEL - 1 - b) if flip else (a, b)
                    tap = kern[at[0], at[1] : at[1] + 1, cols]
                    for q in range(8):
                        acc[q] = acc[q] + rows[q + a] * tap
            for q in range(8):
                emit(top + q, cols, acc[q])
            return carry

        lax.fori_loop(0, 2, lanes, 0)

    def win_part(slot, j):
        return win.at[slot, pl.ds(32 * j, 32)]

    def win_from(t, slot, j):
        return w_in.at[pl.ds(32 * j, 32)] if t == 0 else win_part(slot, j)

    def win_send(far, t, j):
        owner = at_y(-turn * t) if far else at_y(turn * t)
        dev = row_dev(at_y(turn) if far else at_y(-turn), c)
        slot = 2 * owner + c
        return send(
            win_from(t, slot, j), win_part(slot, j), s_w, r_w.at[slot, j], dev,
        )

    def win_share(t, owner, j):
        slot = 2 * owner + c
        return send(
            win_from(t, slot, j), win_part(slot, j), s_w, r_wp, partner
        )

    def win_relay(d, j):
        if d <= long:
            slot = 2 * at_y(-turn * d) + c
            got(win_part(slot, j), r_w.at[slot, j])
            if d < long:
                win_send(True, d, j).start()
            win_share(d, at_y(-turn * d), j).start()
        if d <= short:
            slot = 2 * at_y(turn * d) + c
            got(win_part(slot, j), r_w.at[slot, j])
            if d < short:
                win_send(False, d, j).start()
            win_share(long + d, at_y(turn * d), j).start()

    def zone(zz, cc, j):
        return wo.at[:, j, cc, zz]

    def wo_send(far, t, j):
        owner = at_z(-turn * t) if far else at_z(turn * t)
        dev = {"section": at_z(turn) if far else at_z(-turn)}
        ref = zone(owner, c, j)
        return send(ref, ref, s_z, r_z.at[owner, j], dev)

    def wo_share(t, owner, j):
        ref = zone(owner, c, j)
        return send(ref, ref, s_z, r_zp, partner)

    def wo_relay(d, j):
        if d <= zlong:
            owner = at_z(-turn * d)
            got(zone(owner, c, j), r_z.at[owner, j])
            if d < zlong:
                wo_send(True, d, j).start()
            wo_share(d, owner, j).start()
        if d <= zshort:
            owner = at_z(turn * d)
            got(zone(owner, c, j), r_z.at[owner, j])
            if d < zshort:
                wo_send(False, d, j).start()
            wo_share(zlong + d, owner, j).start()

    right, left = {"col": at_x(1)}, {"col": at_x(nx - 1)}

    def ring_copy(src, ref, parts, ssem, rsem, n):
        part = (0, 1, 1, 0, 0, 1)[n]
        owner = x if n < 4 else (at_x(nx - 1) if n == 4 else at_x(1))
        dst = ref.at[owner, parts[part]]
        return send(
            src.at[parts[part]] if n < 4 and src is not None else dst, dst, ssem,
            rsem.at[min(n, 2)], right if n in (0, 2, 4) else left,
        )

    def ring_relay(ref, parts, ssem, rsem):
        got(ref.at[at_x(nx - 1), parts[0]], rsem.at[0])
        ring_copy(None, ref, parts, ssem, rsem, 4).start()
        got(ref.at[at_x(1), parts[1]], rsem.at[1])
        ring_copy(None, ref, parts, ssem, rsem, 5).start()

    def ring_rest(ref, rsem):
        got(ref.at[pl.ds(0, 2)], rsem.at[2])

    up_parts = (pl.ds(0, 8), pl.ds(8, 8))
    ft_parts = (pl.ds(0, half), pl.ds(half, half + 16))

    my_rows = w_out.at[pl.ds(pl.multiple_of(z * 32, 32), 32), :]

    def slice_send(d):
        return send(my_rows, sl.at[y], s_sl, r_sl, row_dev(at_y(d), c))

    def to_col(src, dst, ssem, rsem, d):
        return send(src, dst, ssem, rsem, {"col": at_x(d)})

    halo_start(0, image_hbm)
    for d in range(1, ny):
        slice_send(d).start()
    for n in range(4):
        ring_copy(up_hbm, ups, up_parts, s_up, r_up, n).start()
    for j in range(2):
        win_send(True, 0, j).start()
        win_send(False, 0, j).start()
        win_share(0, y, j).start()
    local = [
        pltpu.make_async_copy(w_in, win.at[r], s_loc.at[1]),
        pltpu.make_async_copy(my_rows, sl.at[y], s_loc.at[2]),
        pltpu.make_async_copy(up_hbm, ups.at[x], s_loc.at[3]),
    ]
    for copy in local:
        copy.start()
    for copy in loads:
        copy.wait()

    fill(pl.ds(3, 16), pl.ds(8, 16), image[...].astype(F32))
    halo_take(0)

    def keep(i, cols, value):
        mix[i, :, cols] = value

    g_row = gain[...]
    g_high = g_row.astype(BF16).astype(F32)
    tail = lax.broadcasted_iota(jnp.int32, (16, 256), 0)
    feat[x, pl.ds(cells, 16), :] = jnp.where(
        tail == 0, g_high, jnp.where(tail == 1, g_row - g_high, 0.0)
    ).astype(BF16)
    lane = lax.broadcasted_iota(jnp.int32, (half, 128), 1)

    def as_rows(first, second):
        both = jnp.where(lane == 0, first, jnp.where(lane == 1, second, 0.0))
        return both.T[0:8, :]

    stat_own = pl.ds(pl.multiple_of(x * 8, 8), 8)

    def centre_half(p):
        flat = mix[8 * p : 8 * p + 8].reshape(half, 256)
        mean_own = jnp.sum(flat, axis=-1, keepdims=True) * (1.0 / 256)
        centred = flat - mean_own
        square = jnp.sum(centred * centred, axis=-1, keepdims=True)
        feat[x, pl.ds(half * p, half), :] = (centred * g_row).astype(BF16)
        stat[stat_own, pl.ds(half * p, half)] = as_rows(mean_own, square)

    def feat_copy(n):
        return ring_copy(feat.at[x] if n < 4 else None, feat, ft_parts, s_ft, r_ft, n)

    def cross(d):
        dest = at_x(d)
        return send(
            sl.at[pl.ds(2 * dest, 2)], wo.at[x, :, c, z], s_wx, r_wx, {"col": dest}
        )

    others = nx - 1
    stat_bytes = stat.at[pl.ds(0, 8 * others), :]

    ring_relay(ups, up_parts, s_up, r_up)
    conv(False, 0, keep)
    centre_half(0)
    feat_copy(0).start()

    for copy in local:
        copy.wait()
    got(sl.at[pl.ds(0, ny - 1)], r_sl)
    for d in range(1, nx):
        cross(d).start()
    mine = pltpu.make_async_copy(sl.at[pl.ds(2 * x, 2)], wo.at[x, :, c, z], s_loc.at[4])
    mine.start()
    conv(False, 8, keep)
    centre_half(1)
    for d in range(1, nx):
        to_col(stat.at[stat_own, :], stat.at[stat_own, :], s_st, r_st, d).start()
    for n in (1, 2, 3):
        feat_copy(n).start()
    win_relay(1, 0)
    win_relay(1, 1)
    mine.wait()
    got(sl.at[pl.ds(0, 2 * others)], r_wx)
    for j in range(2):
        wo_send(True, 0, j).start()
        wo_send(False, 0, j).start()
        wo_share(0, z, j).start()
    win_relay(2, 0)
    ring_relay(feat, ft_parts, s_ft, r_ft)
    win_relay(2, 1)
    wo_relay(1, 0)
    win_relay(3, 0)
    wo_relay(1, 1)
    win_relay(3, 1)
    wo_relay(2, 0)
    win_relay(4, 0)
    wo_relay(2, 1)
    win_relay(4, 1)

    got(stat_bytes, r_st)
    ring_rest(feat, r_ft)
    got(win.at[pl.ds(0, ny)], r_wp)

    columns = stat[...].T
    means = [columns[:, 8 * k : 8 * k + 1] for k in range(nx)]
    centre = (means[0] + means[1] + means[2] + means[3]) * 0.25
    shifts = [m - centre for m in means]
    total = columns[:, 1:2] + columns[:, 9:10] + columns[:, 17:18] + columns[:, 25:26]
    spread = total + 256.0 * (
        shifts[0] * shifts[0] + shifts[1] * shifts[1] + shifts[2] * shifts[2]
        + shifts[3] * shifts[3]
    )
    inv_std = lax.rsqrt(spread * (1.0 / 1024) + EPSILON)
    for k in range(nx):
        dinv[k] = jnp.broadcast_to(shifts[k] * inv_std, (cells, 128))
    dinv[4] = jnp.broadcast_to(inv_std, (cells, 128))
    dinv[5] = jnp.broadcast_to(centre, (cells, 128))

    def wide(n):
        part = dinv[n]
        return jnp.concatenate([part, part], axis=1)

    def first_product(n, carry):
        cols = pl.ds(pl.multiple_of(n * 256, 256), 256)
        acc = jnp.zeros((cells, 256), F32)
        shift = jnp.zeros((cells, 256), F32)
        gsum = jnp.zeros((1, 256), F32)
        for k in range(nx):
            block = win[4 * k : 4 * k + 4, :, cols].reshape(256, 256)
            part = dot_nn(feat[k], block)
            acc = acc + part[:cells]
            row = part[cells : cells + 1] + part[cells + 1 : cells + 2]
            shift = shift + wide(k) * row
            gsum = gsum + row
        pre[:, cols] = acc * wide(4) + shift
        gws[:, cols] = jnp.broadcast_to(gsum, (8, 256))
        return carry

    lax.fori_loop(0, 2, first_product, 0)
    wo_relay(3, 0)
    lax.fori_loop(2, 4, first_product, 0)

    wo_relay(3, 1)
    for j in range(2):
        wo_relay(4, j)
    ring_rest(ups, r_up)
    got(win.at[pl.ds(0, nz)], r_zp)

    sums[...] = jnp.zeros(sums.shape, F32)

    def activation(n, carry):
        cols = pl.ds(pl.multiple_of(n * 256, 256), 256)
        grad = jnp.zeros((cells, 256), F32)
        for k in range(nx):
            block = wo[k, lax.div(n, 2), lax.rem(n, 2)].reshape(256, 256)
            grad = grad + dot_nt(ups[k].reshape(cells, 256), block)
        value = pre[:, cols]
        phi = 0.5 * (1.0 + lax.erf(value * (1.0 / math.sqrt(2.0))))
        slope = phi + value * jnp.exp(-0.5 * value * value) * (1.0 / math.sqrt(2.0 * math.pi))
        hb[:, cols] = (value * phi).astype(BF16)
        act = (grad * slope).astype(BF16)
        ag[:, cols] = act
        actf = act.astype(F32)
        one = actf * gws[0:1, cols]
        two = actf * value
        sums[0] += one[:, :128] + one[:, 128:]
        sums[1] += two[:, :128] + two[:, 128:]
        return carry

    lax.fori_loop(0, 4, activation, 0)

    def win_block(k):
        return win[pl.ds(pl.multiple_of(k * 4, 4), 4)].reshape(256, 1024)

    for p in range(2):
        rows_of = pl.ds(half * p, half)
        stat2[stat_own, rows_of] = as_rows(
            jnp.sum(sums[0, rows_of, :], axis=-1, keepdims=True),
            jnp.sum(sums[1, rows_of, :], axis=-1, keepdims=True),
        )
    for d in range(1, nx):
        to_col(stat2.at[stat_own, :], stat2.at[stat_own, :], s_s2, r_s2, d).start()

    class Scatter:
        def __init__(self, far, keep_f32, sent, far_got, got_, own, ssem, rsem, product):
            self.far, self.keep, self.sent = far, keep_f32, sent
            self.far_got, self.got, self.own = far_got, got_, own
            self.ssem, self.rsem, self.product = ssem, rsem, product

        def copy(self, n):
            to = right if n in (0, 2, 4) else left
            rows_ = pl.ds(half * (0, 1, 1, 0, 0, 1)[n], half)
            side = n % 2
            if n < 2:
                src, dst = self.far.at[rows_], self.far_got.at[side]
            else:
                src, dst = self.sent.at[side, rows_], self.got.at[side, rows_]
            return send(src, dst, self.ssem, self.rsem.at[min(n, 2)], to)

        def begin(self):
            self.far[...] = self.product(at_x(2)).astype(BF16)

        def near(self):
            value = self.product(at_x(1))
            self.keep[0] = value[:half]
            self.sent[0, half:] = value[half:].astype(BF16)

        def other(self):
            value = self.product(at_x(nx - 1))
            self.keep[1] = value[half:]
            self.sent[1, :half] = value[:half].astype(BF16)

        def relay(self):
            got(self.far_got.at[0], self.rsem.at[0])
            self.sent[0, :half] = (self.keep[0] + self.far_got[0].astype(F32)).astype(BF16)
            self.copy(4).start()
            got(self.far_got.at[1], self.rsem.at[1])
            self.sent[1, half:] = (self.keep[1] + self.far_got[1].astype(F32)).astype(BF16)
            self.copy(5).start()

        def total(self):
            got(self.got, self.rsem.at[2])
            return self.own[...] + self.got[0].astype(F32) + self.got[1].astype(F32)

    grads = Scatter(
        fg2, fgk, fgs, fge, fgr, fgo, s_fg, r_fg, lambda k: dot_nt(ag[...], win_block(k))
    )
    outs = Scatter(
        ob2, obk, obs, obe, obr, obo, s_ob, r_ob,
        lambda k: dot_nn(hb[...], wo[k].reshape(1024, 256)),
    )
    grads.begin()
    grads.copy(0).start()
    grads.copy(1).start()
    grads.near()
    grads.copy(2).start()
    grads.other()
    grads.copy(3).start()
    fgo[...] = grads.product(x)
    outs.begin()
    outs.near()
    outs.other()
    grads.relay()
    for n in range(4):
        outs.copy(n).start()
    obo[...] = outs.product(x)

    got(stat_bytes, r_s2)
    feature = grads.total()
    columns2 = stat2[...].T
    first = (
        columns2[:, 0:1] + columns2[:, 8:9] + columns2[:, 16:17] + columns2[:, 24:25]
    ) * (1.0 / 1024)
    second = (
        columns2[:, 1:2] + columns2[:, 9:10] + columns2[:, 17:18] + columns2[:, 25:26]
    ) * (1.0 / 1024)
    inv_wide = wide(4)
    normed = (mix[...].reshape(cells, 256) - wide(5)) * inv_wide
    mixed_grad = inv_wide * (feature * g_row - first - normed * second)
    mgb[...] = mixed_grad.astype(BF16).reshape(16, 16, 256)
    halo_start(1, mgb)
    fill(pl.ds(3, 16), pl.ds(8, 16), mixed_grad.reshape(16, 16, 256))
    outs.relay()
    halo_take(1)

    def finish(i, cols, value):
        igrad[i, :, cols] = ups[x, i, :, cols].astype(F32) + value

    conv(True, 0, finish)
    conv(True, 8, finish)
    out[...] = (image[...].astype(F32) + outs.total().reshape(16, 16, 256)).astype(BF16)

    for p in range(2):
        left_here(halo_bytes, s_halo.at[p])
    left_here(win.at[pl.ds(0, 2 * ny - 1)], s_w)
    left_here(win.at[pl.ds(0, 2 * nz - 1)], s_z)
    left_here(sl.at[pl.ds(0, ny - 1)], s_sl)
    left_here(sl.at[pl.ds(0, 2 * others)], s_wx)
    left_here(ups.at[pl.ds(0, 3)], s_up)
    left_here(feat.at[pl.ds(0, 3)], s_ft)
    for ssem in (s_fg, s_ob):
        left_here(ups.at[pl.ds(0, 3)], ssem)
    for ssem in (s_st, s_s2):
        left_here(stat_bytes, ssem)


def local(image, conv_kernel, norm_gain, w_in, w_out, upstream):
    nz, nr, nx = lax.axis_size("section"), lax.axis_size("row"), lax.axis_size("col")
    ny = nr // 2
    height, breadth, chan = image.shape
    cells = height * breadth
    vmem = pl.BlockSpec(memory_space=pltpu.VMEM)
    dma = pltpu.SemaphoreType.DMA
    any_ = pl.BlockSpec(memory_space=pl.ANY)
    half = cells // 2
    scatter = [
        pltpu.VMEM((cells, chan), BF16),
        pltpu.VMEM((2, half, chan), F32),
        pltpu.VMEM((2, cells, chan), BF16),
        pltpu.VMEM((2, half, chan), BF16),
        pltpu.VMEM((2, cells, chan), BF16),
        pltpu.VMEM((cells, chan), F32),
    ]
    scratch = [
        pltpu.VMEM((height, breadth, chan), BF16),
        pltpu.VMEM((7, 7, chan), F32),
        pltpu.VMEM((1, chan), F32),
        pltpu.VMEM((2, 2, 16, EDGE, chan), BF16),
        pltpu.VMEM((2, 2, 3, 16, chan), BF16),
        pltpu.VMEM((2, 4, 3, EDGE, chan), BF16),
        pltpu.VMEM((2, 22, 32, 128), F32),
        pltpu.VMEM((height, breadth, chan), F32),
        pltpu.VMEM((nx, cells + 16, chan), BF16),
        pltpu.VMEM((128, cells), F32),
        pltpu.VMEM((128, cells), F32),
        pltpu.VMEM((nx, height, breadth, chan), BF16),
        pltpu.VMEM((nr, 64, 1024), BF16),
        pltpu.VMEM((ny, 32, chan), BF16),
        pltpu.VMEM((nx, 2, 2, nz, 32, chan), BF16),
        pltpu.VMEM((cells, 1024), F32),
        pltpu.VMEM((8, 1024), F32),
        pltpu.VMEM((cells, 1024), BF16),
        pltpu.VMEM((cells, 1024), BF16),
        pltpu.VMEM((2, cells, 128), F32),
        *scatter,
        *scatter,
        pltpu.VMEM((height, breadth, chan), BF16),
        pltpu.VMEM((6, cells, 128), F32),
        dma((2,)), dma((2,)),
        dma, dma((3,)),
        dma, dma,
        dma, dma((3,)),
        dma, dma((nr, 2)), dma,
        dma, dma,
        dma, dma,
        dma, dma((nz, 2)), dma,
        dma, dma((3,)),
        dma, dma,
        dma, dma((3,)),
        dma((8,)),
    ]
    return pl.pallas_call(
        body,
        out_shape=(
            pltpu.VMEM(image.shape, BF16),
            pltpu.VMEM(image.shape, F32),
        ),
        in_specs=[any_] * 6,
        out_specs=(vmem, vmem),
        scratch_shapes=scratch,
        compiler_params=pltpu.CompilerParams(
            collective_id=0, has_side_effects=True, vmem_limit_bytes=60 * 1024 * 1024
        ),
        name="block",
    )(image, conv_kernel, norm_gain.reshape(1, chan), w_in, w_out, upstream)


def solution(mesh):
    in_specs = (
        P("section", "row", "col"),
        P(None, None, "col"),
        P("col"),
        P("row", "col"),
        P("row", "col"),
        P("section", "row", "col"),
    )
    out_specs = (P("section", "row", "col"), P("section", "row", "col"))
    return jax.shard_map(local, mesh=mesh, in_specs=in_specs, out_specs=out_specs, check_vma=False)
```

time: 75.8 us -> 64.1 us (0.85)
  Pallas kernels: 72.7 us -> 62 us
  local copies, waits for them, and re-layouts: 2.32 us -> 1.36 us
    pallas_call x1, Pallas kernels: 72.7 us -> 62 us  [local(): pl.pallas_call(body, out_shape=(pltpu.VMEM(image.shape, BF16), pltpu.VMEM...]
    unnamed x4 -> x2, local copies, waits for them, and re-layouts: 2.32 us -> 1.36 us
where the time goes in v2:
time: 64.1 us; the launch traced here: 64 us
  Pallas kernels  62 us (97%)
  local copies, waits for them, and re-layouts  1.36 us (2%)
    pallas_call x1, Pallas kernels, local(): pl.pallas_call(body, out_shape=(pltpu.VMEM(image.shape, BF16), pltpu.VMEM...  62 us
    unnamed x2, local copies, waits for them, and re-layouts  1.36 us

profile of v2, /device:TPU:1, one launch (start us, length us, event | category | flops | bytes accessed | tf_op | source)
XLA Modules:
  0.0 64.0 jit_solution(12644731713672222444)
XLA Ops:
  0.6 62.0 %block.1 = (bf16[16,16,256]{2,1,0:T(8,128)(2,1)S(1)}, f32[16,16,256]{2,1,0:T(8,128)S(1)}) custom-call(bf16[16,16,256]{2,1,0:T(8,128)(2,1)} %image_hbm.1, f32[7,7,256]{2,1,0:T(8,128)} %kern_hbm.1, f32[1,256]{1,0:T(1,128)} %bitcast.1, bf16[64,1024]{1,0:T(8,128)(2,1)} %w_in.1, bf16[256,256]{1,0:T(8,128)(2,1)} %w_out.1, bf16[16,16,256]{2,1,0:T(8,128)(2,1)} %up_hbm.1), custom_call_target="tpu_custom_call" | custom-call | tf_op jit(solution)/shard_map/block/pallas_call | solution.py:598
  62.6 0.7 %copy.10 = bf16[16,16,256]{2,1,0:T(8,128)(2,1)} copy(bf16[16,16,256]{2,1,0:T(8,128)(2,1)S(1)} %get-tuple-element.2) | data formatting | bytes 262144
  63.3 0.7 %copy.11 = f32[16,16,256]{2,1,0:T(8,128)} copy(f32[16,16,256]{2,1,0:T(8,128)S(1)} %get-tuple-element.3) | data formatting | bytes 524288
